TPU v7x, 256 devices: a whole 4x4x8 slice. The times are simulated.
256 devices in a mesh: row: 16 (over x, y_lo, core), col: 8 (over z), slab: 2 (over y_hi).
Axes of the slice: x: 4, y: 4 (y_hi: 2, y_lo: 2; y = y_hi * 2 + y_lo), z: 8, core: 2. Of those that a mesh axis runs over, the one named last changes fastest.
Arguments:
- fields: bfloat16 [2, 16384, 1024], P(None, ('row', 'col', 'slab')), may hold values from -0.8984375 to 0.8984375
Outputs:
- gram: float32 [2, 16384, 16384], P(None, ('row', 'slab'), 'col')
All inputs are finite; a program needn't handle non-finite values.
Results may differ from a plain program's by a relative error of at most 0.01.
Values may be sent and summed in bfloat16 or wider, within the bound.
A program may use at most 64 MiB of HBM per device.

v0:
```python
import jax
import jax.numpy as jnp
from jax import lax
from jax.sharding import PartitionSpec as P


def pair_terms(left_real, left_imag, piece):
    right_real = jnp.concatenate([piece[0], piece[1]], axis=1)
    right_imag = jnp.concatenate([piece[1], piece[0]], axis=1)
    dims = (((1,), (1,)), ((), ()))
    real = lax.dot_general(left_real, right_real, dims, preferred_element_type=jnp.float32)
    imag = lax.dot_general(left_imag, right_imag, dims, preferred_element_type=jnp.float32)
    return jnp.stack([real, imag])


def body(fields):
    local = lax.all_to_all(fields, "slab", split_axis=2, concat_axis=1, tiled=True)
    row_block = lax.all_gather(local, "col", axis=1, tiled=True)
    left_real = jnp.concatenate([row_block[0], row_block[1]], axis=1)
    left_imag = jnp.concatenate([row_block[0], -row_block[1]], axis=1)
    column_set = lax.all_gather(local, "row", axis=1, tiled=True)
    terms = pair_terms(left_real, left_imag, column_set)
    gram = lax.psum_scatter(
        terms.astype(jnp.bfloat16), "slab", scatter_dimension=1, tiled=True
    ).astype(jnp.float32)
    return gram


def solution(mesh):
    placed = (P(None, ("row", "col", "slab"), None),)
    return jax.shard_map(
        body, mesh=mesh, in_specs=placed, out_specs=P(None, ("row", "slab"), "col"), check_vma=False
    )
```

profile of v0, /device:TPU:24, one launch (start us, length us, event | category | flops | bytes accessed | tf_op | source)
XLA Modules:
  0.0 239.9 jit_solution(3190334933049715580)
XLA Ops:
  6.5 0.0 all-gather.3.cloned.1.call-start
  6.5 1.3 copy.3
  7.8 0.4 reshape
  8.2 8.0 %all_to_all.18 = bf16[2,2,32768]{2,1,0:T(2,128)(2,1)S(1)} all-to-all(bf16[2,2,32768]{2,1,0:T(2,128)(2,1)S(1)} %reshape), channel_id=1, replica_groups=mesh['row'=16,'col'=8,'slab'=2] {'slab'}, dimensions={0} | all-to-all | bytes 524288 | tf_op jit(solution)/shard_map/all_to_all | solution.py:17
  16.2 0.3 reshape.1
  16.6 1.0 copy.5
  17.6 0.0 all-gather.3.cloned.1.call-update
  17.6 0.0 all-gather.5.cloned.1.call-start
  17.7 0.7 all-gather.5.cloned.1.call-update
  18.4 0.0 reduce-scatter.2.cloned.1.call-start
  18.4 43.6 %all-gather.3.cloned.1.call-done = bf16[2,1024,512]{2,1,0:T(8,128)(2,1)} async-done(((bf16[2,128,512]{2,1,0:T(8,128)(2,1)}), bf16[2,1024,512]{2,1,0:T(8,128)(2,1)}) %all-gather.3.cloned.1.call-update) | async-done | bytes 2097168 | tf_op jit(solution)/shard_map/all_gather | solution.py:18
  62.0 1.3 fusion.16
  63.3 2.6 %slice_bitcast_fusion.2 = (bf16[1024,512]{1,0:T(8,128)(2,1)}, bf16[1024,512]{1,0:T(8,128)(2,1)S(1)}) fusion(bf16[2,1024,512]{2,1,0:T(8,128)(2,1)} %all-gather.3.cloned.1.call-done), kind=kLoop, calls=%fused_computation.17 | loop fusion | bytes 4194304 | tf_op jit(solution)/shard_map/squeeze | solution.py:19
  66.0 36.0 %all-gather.5.cloned.1.call-done = bf16[2,2048,512]{2,1,0:T(8,128)(2,1)} async-done(((bf16[2,128,512]{2,1,0:T(8,128)(2,1)}), bf16[2,2048,512]{2,1,0:T(8,128)(2,1)}) %all-gather.5.cloned.1.call-update) | async-done | bytes 4194320 | tf_op jit(solution)/shard_map/all_gather | solution.py:21
  102.0 0.0 copy-start
  102.0 2.6 %slice_bitcast_fusion = (bf16[2048,512]{1,0:T(8,128)(2,1)S(1)}, bf16[2048,512]{1,0:T(8,128)(2,1)S(1)}) fusion(bf16[2,2048,512]{2,1,0:T(8,128)(2,1)} %all-gather.5.cloned.1.call-done), kind=kLoop, calls=%fused_computation.13 | loop fusion | bytes 8388608 | tf_op jit(solution)/shard_map/squeeze | solution.py:8
  104.6 0.0 copy-done
  104.6 4.8 %convert_bitcast_fusion.1 = bf16[1,1024,2048]{2,1,0:T(8,128)(2,1)S(1)} fusion(bf16[2048,512]{1,0:T(8,128)(2,1)S(1)} %get-tuple-element.5, bf16[2048,512]{1,0:T(8,128)(2,1)S(1)} %get-tuple-element.6, bf16[1024,512]{1,0:T(8,128)(2,1)S(1)} %get-tuple-element.8, bf16[1024,512]{1,0:T(8,128)(2,1)S(1)} %copy-done), kind=kOutput, calls=%fused_computation.10 | convolution fusion | flops 4309647360 | bytes 10485760 | tf_op jit(solution)/shard_map/dot_general | solution.py:11
  109.4 6.1 %convert_bitcast_fusion = bf16[1,1024,2048]{2,1,0:T(8,128)(2,1)} fusion(bf16[2048,512]{1,0:T(8,128)(2,1)S(1)} %get-tuple-element.6, bf16[2048,512]{1,0:T(8,128)(2,1)S(1)} %get-tuple-element.5, bf16[1024,512]{1,0:T(8,128)(2,1)S(1)} %get-tuple-element.8, bf16[1024,512]{1,0:T(8,128)(2,1)S(1)} %fusion.16), kind=kOutput, calls=%fused_computation.9 | convolution fusion | flops 4309647360 | bytes 10485760 | tf_op jit(solution)/shard_map/dot_general | solution.py:12
  115.5 6.3 %pad_maximum_fusion = bf16[2,1024,2048]{2,1,0:T(8,128)(2,1)} fusion(bf16[1,1024,2048]{2,1,0:T(8,128)(2,1)} %convert_bitcast_fusion, bf16[1,1024,2048]{2,1,0:T(8,128)(2,1)S(1)} %convert_bitcast_fusion.1), kind=kLoop, calls=%fused_computation | loop fusion | flops 4194304 | bytes 16777216 | tf_op jit(solution)/shard_map/stack | solution.py:13
  121.9 0.0 reduce-scatter.2.cloned.1.call-update
  121.9 104.8 %reduce-scatter.2.cloned.1.call-done = bf16[2,512,2048]{2,1,0:T(8,128)(2,1)} async-done(((bf16[2,1024,2048]{2,1,0:T(8,128)(2,1)}), bf16[2,512,2048]{2,1,0:T(8,128)(2,1)}) %reduce-scatter.2.cloned.1.call-update) | async-done | bytes 4194320 | tf_op jit(solution)/shard_map/reduce_scatter | solution.py:23
  226.7 6.7 %convert_element_type.4 = f32[2,512,2048]{2,1,0:T(8,128)} convert(bf16[2,512,2048]{2,1,0:T(8,128)(2,1)} %reduce-scatter.2.cloned.1.call-done) | non-fusion elementwise | flops 2097152 | bytes 12582912 | tf_op jit(solution)/shard_map/convert_element_type | solution.py:25
Async XLA Ops:
  6.5 55.5 %all-gather.3.cloned.1.call-start = ((), (), s32[]{:S(2)}) async-start(), calls=%async_computation.2 | async-start | bytes 2359296 | tf_op jit(solution)/shard_map/all_gather | solution.py:18
  17.6 84.4 %all-gather.5.cloned.1.call-start = ((), (), s32[]{:S(2)}) async-start(), calls=%async_computation.3 | async-start | bytes 4456448 | tf_op jit(solution)/shard_map/all_gather | solution.py:21
  18.4 208.3 %reduce-scatter.2.cloned.1.call-start = ((), (), s32[]{:S(2)}) async-start(), calls=%async_computation.4 | async-start | bytes 12582912 | tf_op jit(solution)/shard_map/reduce_scatter | solution.py:23
  102.0 2.6 %copy-start = (bf16[1024,512]{1,0:T(8,128)(2,1)S(1)}, bf16[1024,512]{1,0:T(8,128)(2,1)}, u32[]{:S(2)}) copy-start(bf16[1024,512]{1,0:T(8,128)(2,1)} %get-tuple-element.7) | copy-start | bytes 3145732
Sparse Core Ops, SparseCore 0:
  17.7 44.2 all-gather.2
  63.8 38.1 all-gather.4
  122.0 104.6 reduce-scatter.1
where the time goes:
time: 243 us; the launch traced here: 240 us
  waiting for transfers between devices  185 us (76%)
  other arithmetic  14.3 us (6%)
  between operations  13.2 us (5%)
  matrix products  10.9 us (4%)
  local copies, waits for them, and re-layouts  8.25 us (3%)
  blocking collectives  8.02 us (3%)
    reduce_scatter x1, waiting for transfers between devices, body(): lax.psum_scatter(terms.astype(jnp.bfloat16), 'slab', scatter_dimension=1,...  105 us
    all_gather x1, waiting for transfers between devices, body(): row_block = lax.all_gather(local, 'col', axis=1, tiled=True)  43.6 us
    all_gather x1, waiting for transfers between devices, body(): column_set = lax.all_gather(local, 'row', axis=1, tiled=True)  36 us
    all_to_all x1, blocking collectives, body(): lax.all_to_all(fields, 'slab', split_axis=2, concat_axis=1, tiled=True)  8.02 us
    convert_element_type x1, other arithmetic, body(): gram = lax.psum_scatter(terms.astype(jnp.bfloat16), 'slab', scatter_dimen...  6.65 us
    another operation x1, other arithmetic, pair_terms(): return jnp.stack([real, imag])  6.35 us
    dot_general x1, matrix products, pair_terms(): lax.dot_general(left_imag, right_imag, dims, preferred_element_type=jnp.f...  6.13 us
  transfers between devices with their start and end apart: 3, of which 3 were waited for; matrix products, arithmetic and copies ran while one was open for 2% of the time, Pallas kernels for 0%

commit v1 on v0

v1 whole, which is shorter than its diff:
```python
import jax
import jax.numpy as jnp
from jax import lax
from jax.experimental import pallas as pl
from jax.experimental.pallas import tpu as pltpu
from jax.sharding import PartitionSpec as P

MESH = pl.DeviceIdType.MESH
NT = (((1,), (1,)), ((), ()))
STEPS = (0, -1, 1, 2)
ELECTRON_OF_SLOT = (0, 3, 1, 2)


def kernel(f_ref, out_ref, cols, rows, neg, xy_send, xy_recv, d_send, d_recv, z_send, z_recv, own_sem):
    e, half = f_ref.shape[1], f_ref.shape[1] // 2
    r, z, s = lax.axis_index("row"), lax.axis_index("col"), lax.axis_index("slab")
    x, y_lo, core = r // 4, (r // 2) % 2, r % 2
    y = s * 2 + y_lo

    def at(x, y, z, core):
        return (x * 4 + (y % 2) * 2 + core, z, y // 2)

    to = {
        (0, 1): at((x + 1) % 4, y, z, core),
        (0, -1): at((x + 3) % 4, y, z, core),
        (1, 1): at(x, (y + 1) % 4, z, core),
        (1, -1): at(x, (y + 3) % 4, z, core),
        (2, 1): at(x, y, (z + 1) % 8, core),
        (2, -1): at(x, y, (z + 7) % 8, core),
        "core": at(x, y, z, 1 - core),
    }

    barrier = pltpu.get_barrier_semaphore()
    for device in to.values():
        pl.semaphore_signal(barrier, inc=1, device_id=device, device_id_type=MESH)
    pl.semaphore_wait(barrier, len(to))

    def piece(dx, dy):
        px, py = (x + dx + 4) % 4, (y + dy + 4) % 4
        return (px * 4 + (py % 2) * 2 + core) * 2 + py // 2

    def offset(plane, first, second):
        return (first, second) if plane == 0 else (second, first)

    def whole(plane, d):
        return cols.at[plane, piece(*d)]

    def part(plane, d, h):
        return cols.at[plane, piece(*d), pl.ds(h * half, half)]

    def source(plane, d):
        return f_ref.at[plane] if d == (0, 0) else whole(plane, d)

    def xy_copy(src, dst, device, index):
        return pltpu.make_async_remote_copy(
            src_ref=src, dst_ref=dst, send_sem=xy_send.at[0], recv_sem=xy_recv.at[index],
            device_id=device, device_id_type=MESH,
        )

    def send_whole(plane, d, axis, way, group):
        xy_copy(source(plane, d), whole(plane, d), to[(axis, way)], (plane * 5 + group) * 4 + (0 if way == 1 else 1)).start()

    def send_part(plane, d, h, axis, way, group):
        xy_copy(part(plane, d, h), part(plane, d, h), to[(axis, way)], (plane * 5 + group) * 4 + 2 + h).start()

    def hand_over(plane, d):
        pltpu.make_async_remote_copy(
            src_ref=source(plane, d), dst_ref=whole(plane, d), send_sem=d_send.at[0], recv_sem=d_recv.at[d[0] % 4],
            device_id=to["core"], device_id_type=MESH,
        ).start()

    def first_axis(plane):
        return 0 if plane == 0 else 1

    def spread(plane, i):
        d = offset(plane, STEPS[i], 0)
        for way in (1, -1):
            send_whole(plane, d, 1 - first_axis(plane), way, 1 + i)

    def take_wholes(plane, group):
        axis = first_axis(plane) if group == 0 else 1 - first_axis(plane)
        for kind, way in ((0, 1), (1, -1)):
            d = offset(plane, -way, 0) if group == 0 else offset(plane, STEPS[group - 1], -way)
            xy_copy(whole(plane, d), whole(plane, d), to["core"], (plane * 5 + group) * 4 + kind).wait_recv()
            send_part(plane, d, kind, axis, way, group)
            hand_over(plane, d)

    def take_parts(plane, group):
        d = offset(plane, 2, 0) if group == 0 else offset(plane, STEPS[group - 1], 2)
        for h in (0, 1):
            xy_copy(part(plane, d, h), part(plane, d, h), to["core"], (plane * 5 + group) * 4 + 2 + h).wait_recv()
        hand_over(plane, d)

    j = (z - 4 * s + 8) % 8
    places = (j, (11 - j) % 8)

    def slot_of(source_electron):
        c = source_electron
        return c + (c + 2) // 3 - 3 * (c // 3)

    def z_copy(way, n, src, dst, a):
        return pltpu.make_async_remote_copy(
            src_ref=src, dst_ref=dst, send_sem=z_send.at[way * 2 + a], recv_sem=z_recv.at[way * 16 + n],
            device_id=to[(2, 1 if way == 0 else -1)], device_id_type=MESH,
        )

    def rows_part(plane, other, slot, h):
        return rows.at[plane, other * 4 + slot, pl.ds(pl.multiple_of(h * half, half), half)]

    def z_own(other, parts):
        for way in (0, 1):
            @pl.when(places[way] < 4)
            def _():
                for i in parts:
                    plane, h = 1 - i // 2, i % 2
                    src = f_ref.at[plane, pl.ds(h * half, half)] if other == 0 else part(plane, (0, 2), h)
                    z_copy(way, other * 8 + i, src, rows_part(plane, other, slot_of(j), h), 0).start()

    def z_step(slot):
        for way in (0, 1):
            place = places[way]
            back = (place + 7) % 8
            far = back // 4
            n = slot - 2 * far * (back - 3) + (2 * (back // 7) if slot >= 14 else 0)
            other, a, i = n // 8, (n // 4) % 2, n % 4
            plane, h = 1 - i // 2, i % 2

            @pl.when((n >= 0) & (n < 16) & ((a == 0) | (place >= 2)))
            def _():
                origin = back - far * (back - 3) - a
                electron = origin if way == 0 else 3 - origin
                block = rows_part(plane, other, slot_of(electron), h)
                z_copy(way, n, block, block, 0).wait_recv()

                @pl.when((place >= 4) & (a == 0))
                def _():
                    z_copy(way, n, block, block, 0).start()

                @pl.when((place >= 4) & (place <= 6) & (a == 1))
                def _():
                    z_copy(way, n, block, block, 1).start()

                @pl.when((place >= 1) & (place <= 3) & (a == 0))
                def _():
                    z_copy(way, n + 4, block, block, 1).start()

    def wait_columns(dx):
        pltpu.make_async_copy(cols.at[0, pl.ds(0, 8)], cols.at[0, pl.ds(0, 8)], d_recv.at[dx % 4]).wait()

    def negate(slot, count):
        neg[pl.ds(slot, count)] = -rows[1, pl.ds(slot, count)]

    def multiply(slot, count, dx, start, width):
        m = count * e
        first = ((x + dx + 4) % 4) * 8 + start
        right_re = cols[0, pl.ds(first, width)].reshape(width * e, -1)
        right_im = cols[1, pl.ds(first, width)].reshape(width * e, -1)
        left_re = rows[0, pl.ds(slot, count)].reshape(m, -1)
        left_im = rows[1, pl.ds(slot, count)].reshape(m, -1)
        minus_im = neg[pl.ds(slot, count)].reshape(m, -1)
        sums = lax.dot_general(
            jnp.concatenate([left_re, minus_im]), right_re, NT, preferred_element_type=jnp.float32
        ) + lax.dot_general(jnp.concatenate([left_im, left_re]), right_im, NT, preferred_element_type=jnp.float32)
        lanes = pl.ds(pl.multiple_of(first * e, 128), width * e)
        for i in range(count):
            other, electron = (slot + i) // 4, ELECTRON_OF_SLOT[(slot + i) % 4]
            low = pl.multiple_of(electron * 2 * e + (s if other == 0 else 1 - s) * e, e)
            for plane in (0, 1):
                out_ref[plane, pl.ds(low, e), lanes] = sums[plane * m + i * e : plane * m + (i + 1) * e]

    here = (0, 0)
    z_own(0, (0, 1, 2, 3))
    for plane in (0, 1):
        for way in (1, -1):
            send_whole(plane, here, first_axis(plane), way, 0)
    for plane in (0, 1):
        spread(plane, 0)
    for plane in (0, 1):
        hand_over(plane, here)
    own = [pltpu.make_async_copy(f_ref.at[plane], whole(plane, here), own_sem.at[plane]) for plane in (0, 1)]
    for copy in own:
        copy.start()

    @pl.when(j < 4)
    def _():
        for plane in (0, 1):
            rows[plane, slot_of(j)] = f_ref[plane]

    z_step(0)
    z_step(1)
    for plane in (0, 1):
        take_wholes(plane, 0)
    for plane in (0, 1):
        spread(plane, 1)
    z_step(2)
    z_step(3)
    for plane in (0, 1):
        take_wholes(plane, 1)
    for plane in (0, 1):
        spread(plane, 2)
    z_step(4)
    for plane in (0, 1):
        take_parts(plane, 0)
    z_own(1, (0, 1))
    for plane in (0, 1):
        spread(plane, 3)
    z_step(5)
    z_step(6)
    for plane in (0, 1):
        take_wholes(plane, 2)
    z_step(7)
    for plane in (0, 1):
        take_parts(plane, 1)
    z_own(1, (2, 3))

    @pl.when(j < 4)
    def _():
        for plane in (0, 1):
            rows[plane, 4 + slot_of(j)] = cols[plane, piece(0, 2)]

    z_step(8)
    z_step(9)
    for plane in (0, 1):
        take_wholes(plane, 3)
    z_step(10)
    z_step(11)
    for plane in (0, 1):
        take_wholes(plane, 4)
    z_step(12)
    for plane in (0, 1):
        take_parts(plane, 2)
    z_step(13)
    for plane in (0, 1):
        take_parts(plane, 3)
    for copy in own:
        copy.wait()
    negate(0, 4)
    wait_columns(0)
    multiply(0, 4, 0, 0, 4)
    z_step(14)
    for plane in (0, 1):
        take_parts(plane, 4)
    multiply(0, 4, 0, 4, 4)
    for i, dx in ((1, -1), (2, 1), (3, 2)):
        z_step(14 + i)
        wait_columns(dx)
        multiply(0, 4, dx, 0, 4)
        multiply(0, 4, dx, 4, 4)
    negate(4, 2)
    for i, dx in enumerate(STEPS):
        z_step(18 + i)
        multiply(4, 2, dx, 0, 8)
    negate(6, 2)
    for dx in STEPS:
        multiply(6, 2, dx, 0, 8)

    def drain(blocks, sem):
        pltpu.make_async_copy(cols.at[0, pl.ds(0, blocks)], cols.at[0, pl.ds(0, blocks)], sem).wait()

    drain(30, xy_send.at[0])
    drain(32, d_send.at[0])
    for way in (0, 1):
        drain(4, z_send.at[way * 2])

        @pl.when((places[way] >= 1) & (places[way] <= 6))
        def _():
            drain(4, z_send.at[way * 2 + 1])


def body(fields):
    e, pixels = fields.shape[1], fields.shape[2]
    return pl.pallas_call(
        kernel,
        out_shape=jax.ShapeDtypeStruct((2, 8 * e, 32 * e), jnp.float32),
        in_specs=[pl.BlockSpec(memory_space=pltpu.VMEM)],
        out_specs=pl.BlockSpec(memory_space=pltpu.VMEM),
        scratch_shapes=[
            pltpu.VMEM((2, 32, e, pixels), jnp.bfloat16),
            pltpu.VMEM((2, 8, e, pixels), jnp.bfloat16),
            pltpu.VMEM((8, e, pixels), jnp.bfloat16),
            pltpu.SemaphoreType.DMA((1,)),
            pltpu.SemaphoreType.DMA((40,)),
            pltpu.SemaphoreType.DMA((1,)),
            pltpu.SemaphoreType.DMA((4,)),
            pltpu.SemaphoreType.DMA((4,)),
            pltpu.SemaphoreType.DMA((32,)),
            pltpu.SemaphoreType.DMA((2,)),
        ],
        compiler_params=pltpu.CompilerParams(collective_id=0, has_side_effects=True, vmem_limit_bytes=56 * 2**20),
        cost_estimate=pl.CostEstimate(flops=8 * 8 * e * 32 * e * pixels, bytes_accessed=2**23, transcendentals=0),
    )(fields)


def solution(mesh):
    placed = (P(None, ("row", "col", "slab"), None),)
    return jax.shard_map(
        body, mesh=mesh, in_specs=placed, out_specs=P(None, ("row", "slab"), "col"), check_vma=False
    )
```

time: 243 us -> 63 us (0.26)
  waiting for transfers between devices: 185 us -> 0 us
  Pallas kernels: 0 us -> 54.2 us
  other arithmetic: 14.3 us -> 0 us
  between operations: 13.2 us -> 0.01 us
  matrix products: 10.9 us -> 0 us
  blocking collectives: 8.02 us -> 0 us
    reduce_scatter x1 -> x0, waiting for transfers between devices: 105 us -> none  [body(): lax.psum_scatter(terms.astype(jnp.bfloat16), 'slab', scatter_dimension=1,...]
    all_gather x2 -> x0, waiting for transfers between devices: 79.6 us -> none  [the longest x1 43.6 us: body(): row_block = lax.all_gather(local, 'col', axis=1, tiled=True)]
    pallas_call x0 -> x1, Pallas kernels: none -> 54.2 us  [body(): pl.pallas_call(kernel, out_shape=jax.ShapeDtypeStruct((2, 8 * e, 32 * e),...]
    dot_general x2 -> x0, matrix products: 10.9 us -> none  [the longest x1 6.13 us: pair_terms(): lax.dot_general(left_imag, right_imag, dims, preferred_element_type=jnp.f...]
    all_to_all x1 -> x0, blocking collectives: 8.02 us -> none  [body(): lax.all_to_all(fields, 'slab', split_axis=2, concat_axis=1, tiled=True)]
    convert_element_type x1 -> x0, other arithmetic: 6.65 us -> none  [body(): gram = lax.psum_scatter(terms.astype(jnp.bfloat16), 'slab', scatter_dimen...]
    another operation x1 -> x0, other arithmetic: 6.35 us -> none  [pair_terms(): return jnp.stack([real, imag])]
    unnamed x5 -> x1, local copies, waits for them, and re-layouts: 2.01 us -> 7.89 us
  transfers between devices with their start and end apart: 3 -> 0, of which waited for: 3 -> 0; matrix products, arithmetic and copies ran while one was open for 2% -> 0% of each run, Pallas kernels for 0% -> 0%
where the time goes in v1:
time: 63 us; the launch traced here: 62.1 us
  Pallas kernels  54.2 us (86%)
  local copies, waits for them, and re-layouts  7.89 us (13%)
    pallas_call x1, Pallas kernels, body(): pl.pallas_call(kernel, out_shape=jax.ShapeDtypeStruct((2, 8 * e, 32 * e),...  54.2 us
    unnamed x1, local copies, waits for them, and re-layouts  7.89 us

profile of v1, /device:TPU:24, one launch (start us, length us, event | category | flops | bytes accessed | tf_op | source)
XLA Modules:
  0.0 62.1 jit_solution(11219425451840442713)
XLA Ops:
  0.0 54.2 %shard_map.17 = f32[2,512,2048]{2,1,0:T(8,128)} custom-call(bf16[2,64,1024]{2,1,0:T(8,128)(2,1)} %f_ref.1), custom_call_target="tpu_custom_call" | custom-call | flops 8589934592 | bytes 8388608 | tf_op jit(solution)/shard_map/pallas_call | solution.py:272
  54.2 7.9 %copy.3 = f32[2,512,2048]{2,1,0:T(8,128)} copy(f32[2,512,2048]{2,1,0:T(8,128)} %shard_map.17) | data formatting | bytes 16777216

commit v2 on v1

v2 whole, which is shorter than its diff:
```python
import jax
import jax.numpy as jnp
from jax import lax
from jax.experimental import pallas as pl
from jax.experimental.pallas import tpu as pltpu
from jax.sharding import PartitionSpec as P

MESH = pl.DeviceIdType.MESH
NT = (((1,), (1,)), ((), ()))
STEPS = (0, -1, 1, 2)
ELECTRON_OF_SLOT = (0, 3, 1, 2)
UNIT = 4
TAIL = 2
DIRECT = 1
SHIFT = (5, 2)
FIRST = {"wholes": (1, 3, 6, 9, 11), "parts": (4, 7, 9, 12, 14), "fourth": 6, "negate": (10, 14, 18)}
PRODUCTS = {
    10: ((0, 2, 0),), 14: ((2, 2, 0),), 15: ((0, 4, -1),), 16: ((0, 4, 1),), 17: ((0, 4, 2),),
    18: ((4, 2, 0),), 19: ((4, 2, -1),), 20: ((4, 2, 1),), 21: ((4, 2, 2),),
}


def is_end(place):
    return (1 - place // 4) * (1 - place * (3 - place) // 2)


def gather_kernel(f_ref, cols, rows, acc, neg, xy_send, xy_recv, d_send, d_recv, z_send, z_recv, z_tail, own_sem):
    e, half, quarter = f_ref.shape[1], f_ref.shape[1] // 2, f_ref.shape[1] * 2 // UNIT
    r, z, s = lax.axis_index("row"), lax.axis_index("col"), lax.axis_index("slab")
    x, y_lo, core = r // 4, (r // 2) % 2, r % 2
    y = s * 2 + y_lo

    def at(x, y, z, core):
        return (x * 4 + (y % 2) * 2 + core, z, y // 2)

    to = {
        (0, 1): at((x + 1) % 4, y, z, core),
        (0, -1): at((x + 3) % 4, y, z, core),
        (1, 1): at(x, (y + 1) % 4, z, core),
        (1, -1): at(x, (y + 3) % 4, z, core),
        (2, 1): at(x, y, (z + 1) % 8, core),
        (2, 2): at(x, y, (z + 2) % 8, core),
        (2, 3): at(x, y, (z + 3) % 8, core),
        (2, 4): at(x, y, (z + 4) % 8, core),
        (2, -1): at(x, y, (z + 7) % 8, core),
        (2, -2): at(x, y, (z + 6) % 8, core),
        (2, -3): at(x, y, (z + 5) % 8, core),
        "core": at(x, y, z, 1 - core),
    }

    barrier = pltpu.get_barrier_semaphore()
    for device in to.values():
        pl.semaphore_signal(barrier, inc=1, device_id=device, device_id_type=MESH)
    pl.semaphore_wait(barrier, len(to))

    def piece(dx, dy):
        px, py = (x + dx + 4) % 4, (y + dy + 4) % 4
        return (px * 4 + (py % 2) * 2 + core) * 2 + py // 2

    def offset(plane, first, second):
        return (first, second) if plane == 0 else (second, first)

    def whole(plane, d):
        return cols.at[plane, piece(*d)]

    def part(plane, d, h):
        return cols.at[plane, piece(*d), pl.ds(h * half, half)]

    def source(plane, d):
        return f_ref.at[plane] if d == (0, 0) else whole(plane, d)

    def xy_copy(src, dst, device, index):
        return pltpu.make_async_remote_copy(
            src_ref=src, dst_ref=dst, send_sem=xy_send.at[0], recv_sem=xy_recv.at[index],
            device_id=device, device_id_type=MESH,
        )

    def send_whole(plane, d, axis, way, group):
        xy_copy(source(plane, d), whole(plane, d), to[(axis, way)], (plane * 5 + group) * 4 + (0 if way == 1 else 1)).start()

    def send_part(plane, d, h, axis, way, group):
        xy_copy(part(plane, d, h), part(plane, d, h), to[(axis, way)], (plane * 5 + group) * 4 + 2 + h).start()

    def hand_over(plane, d):
        pltpu.make_async_remote_copy(
            src_ref=source(plane, d), dst_ref=whole(plane, d), send_sem=d_send.at[0], recv_sem=d_recv.at[d[0] % 4],
            device_id=to["core"], device_id_type=MESH,
        ).start()

    def first_axis(plane):
        return 0 if plane == 0 else 1

    def spread(plane, i):
        d = offset(plane, STEPS[i], 0)
        for way in (1, -1):
            send_whole(plane, d, 1 - first_axis(plane), way, 1 + i)

    def take_wholes(plane, group):
        axis = first_axis(plane) if group == 0 else 1 - first_axis(plane)
        for kind, way in ((0, 1), (1, -1)):
            d = offset(plane, -way, 0) if group == 0 else offset(plane, STEPS[group - 1], -way)
            xy_copy(whole(plane, d), whole(plane, d), to["core"], (plane * 5 + group) * 4 + kind).wait_recv()
            send_part(plane, d, kind, axis, way, group)
            hand_over(plane, d)

    def take_parts(plane, group):
        d = offset(plane, 2, 0) if group == 0 else offset(plane, STEPS[group - 1], 2)
        for h in (0, 1):
            xy_copy(part(plane, d, h), part(plane, d, h), to["core"], (plane * 5 + group) * 4 + 2 + h).wait_recv()
        hand_over(plane, d)

    j = (z - 4 * s + 8) % 8
    places = (j, (11 - j) % 8)

    def slot_of(c, place):
        return (c + (c + 2) // 3 - 3 * (c // 3) + 2 * is_end(place)) % 4

    def z_copy(way, n, src, dst, sem, hops=1):
        return pltpu.make_async_remote_copy(
            src_ref=src, dst_ref=dst, send_sem=sem, recv_sem=z_recv.at[way * 4 * UNIT + n],
            device_id=to[(2, hops if way == 0 or hops == 4 else -hops)], device_id_type=MESH,
        )

    def rows_part(plane, other, slot, q):
        return rows.at[plane, other * 4 + slot, pl.ds(pl.multiple_of(q * quarter, quarter), quarter)]

    def there(way, hops):
        return (j + (hops if way == 0 else 8 - hops)) % 8

    def z_own(other, planes):
        for way in (0, 1):
            @pl.when(places[way] < 4)
            def _():
                for i in range(UNIT):
                    plane, q = 1 - i // (UNIT // 2), i % (UNIT // 2)
                    if plane in planes:
                        src = f_ref.at[plane] if other == 0 else whole(plane, (0, 2))
                        z_copy(
                            way, other * 2 * UNIT + i, src.at[pl.ds(q * quarter, quarter)],
                            rows_part(plane, other, slot_of(j, there(way, 1)), q), z_send.at[way * 2],
                        ).start()

    def z_step(slot):
        last, direct = 4 * UNIT - TAIL, 4 * UNIT - DIRECT
        for way in (0, 1):
            place = places[way]
            back = (place + 7) % 8
            far = back // 4
            n = slot - SHIFT[0] * far * (back - 3) // SHIFT[1]
            other, a, i = n // (2 * UNIT), (n // UNIT) % 2, n % UNIT
            plane, q = 1 - i // (UNIT // 2), i % (UNIT // 2)

            @pl.when((n >= 0) & (n < 4 * UNIT) & ((a == 0) | (place >= 2)))
            def _():
                origin = back - far * (back - 3) - a
                electron = origin if way == 0 else 3 - origin
                block = rows_part(plane, other, slot_of(electron, j), q)
                z_copy(way, n, block, block, z_send.at[0]).wait_recv()

                def send(n, sem, hops=1):
                    to_block = rows_part(plane, other, slot_of(electron, there(way, hops)), q)
                    z_copy(way, n, block, to_block, sem, hops).start()

                @pl.when((place >= 4) & (a == 0))
                def _():
                    send(n, z_send.at[way * 2])

                @pl.when((place >= 4) & (place <= 6) & (a == 1) & (n < last))
                def _():
                    send(n, z_send.at[way * 2 + 1])

                @pl.when((place >= 1) & (place <= 3) & (a == 0) & ((place < 3) | (n < last - UNIT)))
                def _():
                    send(n + UNIT, z_send.at[way * 2 + 1])

                if slot >= last - UNIT:

                    @pl.when(((place == 4) | (place == 6)) & (n >= last) & (n < direct))
                    def _():
                        send(n, z_tail.at[way])

                    @pl.when((place == 3) & (a == 0) & (n >= last - UNIT))
                    def _():
                        send(n + UNIT, z_tail.at[way])
                        send(n + UNIT, z_tail.at[way], 3)

                        @pl.when(n >= direct - UNIT)
                        def _():
                            send(n + UNIT, z_tail.at[way], 2)
                            send(n + UNIT, z_tail.at[way], 4)

    def wait_columns(dx):
        pltpu.make_async_copy(cols.at[0, pl.ds(0, 8)], cols.at[0, pl.ds(0, 8)], d_recv.at[dx % 4]).wait()

    def negate(slot, count):
        neg[pl.ds(slot, count)] = -rows[1, pl.ds(slot, count)]

    def multiply(slot, count, dx, start, width):
        m = count * e
        first = ((x + dx + 4) % 4) * 8 + start
        right_re = cols[0, pl.ds(first, width)].reshape(width * e, -1)
        right_im = cols[1, pl.ds(first, width)].reshape(width * e, -1)
        left_re = rows[0, pl.ds(slot, count)].reshape(m, -1)
        left_im = rows[1, pl.ds(slot, count)].reshape(m, -1)
        minus_im = neg[pl.ds(slot, count)].reshape(m, -1)
        sums = lax.dot_general(
            jnp.concatenate([left_re, minus_im]), right_re, NT, preferred_element_type=jnp.float32
        ) + lax.dot_general(jnp.concatenate([left_im, left_re]), right_im, NT, preferred_element_type=jnp.float32)
        lanes = pl.ds(pl.multiple_of(first * e, 128), width * e)
        for plane in (0, 1):
            acc[plane, slot * e : slot * e + m, lanes] = sums[plane * m : (plane + 1) * m]

    def own_rows(plane):
        return pltpu.make_async_copy(f_ref.at[plane], rows.at[plane, slot_of(j, j)], own_sem.at[2 + plane])

    here = (0, 0)
    both = (0, 1)
    z_own(0, both)
    for plane in both:
        for way in (1, -1):
            send_whole(plane, here, first_axis(plane), way, 0)
    for plane in both:
        spread(plane, 0)
    for plane in both:
        hand_over(plane, here)
    own = [pltpu.make_async_copy(f_ref.at[plane], whole(plane, here), own_sem.at[plane]) for plane in both]
    for copy in own:
        copy.start()

    @pl.when(j < 4)
    def _():
        for plane in both:
            own_rows(plane).start()

    seen = set()

    def after(slot):
        if slot == FIRST["parts"][0]:
            for plane in both:
                take_parts(plane, 0)
            z_own(1, (1,))
        if slot in FIRST["wholes"]:
            group = FIRST["wholes"].index(slot)
            for plane in both:
                take_wholes(plane, group)
            if group < 2:
                for plane in both:
                    spread(plane, 1 + group)
        if slot == FIRST["fourth"]:
            for plane in both:
                spread(plane, 3)
        if slot in FIRST["parts"][1:]:
            group = FIRST["parts"].index(slot)
            for plane in both:
                take_parts(plane, group)
            if group == 1:
                z_own(1, (0,))

                @pl.when(j < 4)
                def _():
                    for plane in both:
                        rows[plane, 4 + slot_of(j, j)] = cols[plane, piece(0, 2)]

        if slot == FIRST["negate"][0]:
            for copy in own:
                copy.wait()

            @pl.when(j < 4)
            def _():
                for plane in both:
                    own_rows(plane).wait()

        if slot in FIRST["negate"]:
            negate(2 * FIRST["negate"].index(slot), 2)
        for low, count, dx in PRODUCTS.get(slot, ()):
            if dx not in seen:
                seen.add(dx)
                wait_columns(dx)
            multiply(low, count, dx, 0, 8)

    for slot in range(4 * UNIT + 3 * SHIFT[0] // SHIFT[1]):
        z_step(slot)
        after(slot)

    def drain(blocks, sem):
        pltpu.make_async_copy(cols.at[0, pl.ds(0, blocks)], cols.at[0, pl.ds(0, blocks)], sem).wait()

    drain(30, xy_send.at[0])
    drain(32, d_send.at[0])
    for way in (0, 1):
        drain(4, z_send.at[way * 2])

        @pl.when((places[way] == 1) | (places[way] == 2))
        def _():
            drain(4, z_send.at[way * 2 + 1])

        @pl.when((places[way] >= 3) & (places[way] <= 6))
        def _():
            drain(3, z_send.at[way * 2 + 1])

        @pl.when(places[way] == 3)
        def _():
            drain(3, z_tail.at[way])

        @pl.when((places[way] == 4) | (places[way] == 6))
        def _():
            pltpu.make_async_copy(part(0, here, 0), part(0, here, 0), z_tail.at[way]).wait()


def finish_kernel(cols, rows, acc, out, neg, last, acc_sem, last_sem):
    e = rows.shape[2]
    s = lax.axis_index("slab")

    at_end = is_end((lax.axis_index("col") - 4 * s + 8) % 8)

    def place(slot):
        side = s if slot < 4 else 1 - s
        plain, turned = ELECTRON_OF_SLOT[slot % 4], ELECTRON_OF_SLOT[(slot + 2) % 4]
        electron = plain + at_end * (turned - plain)
        return pl.ds(pl.multiple_of((electron * 2 + side) * e, e), e)

    copies = []
    for slot in range(6):
        for plane in (0, 1):
            copies.append(pltpu.make_async_copy(
                acc.at[plane, pl.ds(slot * e, e)], out.at[plane, place(slot)], acc_sem.at[slot * 2 + plane]
            ))
            copies[-1].start()
    m = 2 * e
    neg[...] = -rows[1, 6:8]
    left = jnp.concatenate([rows[0, 6:8].reshape(m, -1), neg[...].reshape(m, -1)])
    cross = jnp.concatenate([rows[1, 6:8].reshape(m, -1), rows[0, 6:8].reshape(m, -1)])
    for block in range(4):
        right_re = cols[0, block * 8 : block * 8 + 8].reshape(8 * e, -1)
        right_im = cols[1, block * 8 : block * 8 + 8].reshape(8 * e, -1)
        sums = lax.dot_general(left, right_re, NT, preferred_element_type=jnp.float32) + lax.dot_general(
            cross, right_im, NT, preferred_element_type=jnp.float32
        )
        for plane in (0, 1):
            last[plane, :, block * 8 * e : (block + 1) * 8 * e] = sums[plane * m : (plane + 1) * m]
            for i in (0, 1):
                lanes = pl.ds(block * 8 * e, 8 * e)
                copies.append(pltpu.make_async_copy(
                    last.at[plane, pl.ds(i * e, e), lanes], out.at[plane, place(6 + i), lanes],
                    last_sem.at[block * 4 + plane * 2 + i],
                ))
                copies[-1].start()
    for copy in copies:
        copy.wait()


def body(fields):
    e, pixels = fields.shape[1], fields.shape[2]
    vmem = pltpu.MemorySpace.VMEM
    cols, rows, acc = pl.pallas_call(
        gather_kernel,
        out_shape=(
            pltpu.VMEM((2, 32, e, pixels), jnp.bfloat16),
            pltpu.VMEM((2, 8, e, pixels), jnp.bfloat16),
            pltpu.VMEM((2, 6 * e, 32 * e), jnp.float32),
        ),
        in_specs=[pl.BlockSpec(memory_space=pltpu.MemorySpace.HBM)],
        out_specs=(pl.BlockSpec(memory_space=pltpu.VMEM),) * 3,
        scratch_shapes=[
            pltpu.VMEM((8, e, pixels), jnp.bfloat16),
            pltpu.SemaphoreType.DMA((1,)),
            pltpu.SemaphoreType.DMA((40,)),
            pltpu.SemaphoreType.DMA((1,)),
            pltpu.SemaphoreType.DMA((4,)),
            pltpu.SemaphoreType.DMA((4,)),
            pltpu.SemaphoreType.DMA((8 * UNIT,)),
            pltpu.SemaphoreType.DMA((2,)),
            pltpu.SemaphoreType.DMA((4,)),
        ],
        compiler_params=pltpu.CompilerParams(collective_id=0, has_side_effects=True, vmem_limit_bytes=20 * 2**20),
        cost_estimate=pl.CostEstimate(flops=6 * 8 * e * 32 * e * pixels, bytes_accessed=2**23, transcendentals=0),
    )(pltpu.with_memory_space_constraint(fields, pltpu.MemorySpace.HBM))
    cols, rows, acc = (pltpu.with_memory_space_constraint(a, vmem) for a in (cols, rows, acc))
    return pl.pallas_call(
        finish_kernel,
        out_shape=jax.ShapeDtypeStruct((2, 8 * e, 32 * e), jnp.float32),
        in_specs=[pl.BlockSpec(memory_space=pltpu.VMEM)] * 3,
        out_specs=pl.BlockSpec(memory_space=pl.ANY),
        scratch_shapes=[
            pltpu.VMEM((2, e, pixels), jnp.bfloat16),
            pltpu.VMEM((2, 2 * e, 32 * e), jnp.float32),
            pltpu.SemaphoreType.DMA((12,)),
            pltpu.SemaphoreType.DMA((16,)),
        ],
        compiler_params=pltpu.CompilerParams(vmem_limit_bytes=20 * 2**20),
        cost_estimate=pl.CostEstimate(flops=2 * 8 * e * 32 * e * pixels, bytes_accessed=2**23, transcendentals=0),
    )(cols, rows, acc)


def solution(mesh):
    placed = (P(None, ("row", "col", "slab"), None),)
    return jax.shard_map(
        body, mesh=mesh, in_specs=placed, out_specs=P(None, ("row", "slab"), "col"), check_vma=False
    )
```

time: 63 us -> 52.8 us (0.84); the launches traced: 62.1 us -> 52.7 us
  local copies, waits for them, and re-layouts: 7.89 us -> 0 us
  Pallas kernels: 54.2 us -> 52.6 us
    unnamed x1 -> x0, local copies, waits for them, and re-layouts: 7.89 us -> none
    pallas_call x1 -> x2, Pallas kernels: 54.2 us -> 52.6 us  [the longest x1 48.4 us: body(): pl.pallas_call(gather_kernel, out_shape=(pltpu.VMEM((2, 32, e, pixels), j...]
where the time goes in v2:
time: 52.8 us; the launch traced here: 52.7 us
  Pallas kernels  52.6 us (100%)
    pallas_call x1, Pallas kernels, body(): pl.pallas_call(gather_kernel, out_shape=(pltpu.VMEM((2, 32, e, pixels), j...  48.4 us
    pallas_call x1, Pallas kernels, body(): pl.pallas_call(finish_kernel, out_shape=jax.ShapeDtypeStruct((2, 8 * e, 3...  4.11 us

profile of v2, /device:TPU:24, one launch (start us, length us, event | category | flops | bytes accessed | tf_op | source)
XLA Modules:
  0.0 52.7 jit_solution(11321687762465368565)
XLA Ops:
  0.0 48.4 %shard_map.17 = (bf16[2,32,64,1024]{3,2,1,0:T(8,128)(2,1)S(1)}, bf16[2,8,64,1024]{3,2,1,0:T(8,128)(2,1)S(1)}, f32[2,384,2048]{2,1,0:T(8,128)S(1)}) custom-call(bf16[2,64,1024]{2,1,0:T(8,128)(2,1)} %f_ref.1), custom_call_target="tpu_custom_call" | custom-call | flops 6442450944 | bytes 8388608 | tf_op jit(solution)/shard_map/pallas_call | solution.py:355
  48.4 4.1 %shard_map.18 = f32[2,512,2048]{2,1,0:T(8,128)} custom-call(bf16[2,32,64,1024]{3,2,1,0:T(8,128)(2,1)S(1)} %get-tuple-element.8.cols, bf16[2,8,64,1024]{3,2,1,0:T(8,128)(2,1)S(1)} %get-tuple-element.9.rows, f32[2,384,2048]{2,1,0:T(8,128)S(1)} %get-tuple-element.10.acc), custom_call_target="tpu_custom_call" | custom-call | flops 2147483648 | bytes 8388608 | tf_op jit(solution)/shard_map/pallas_call | solution.py:379

commit v3 on v2

--- a/solution.py
+++ b/solution.py
@@ -10,8 +10,6 @@
 STEPS = (0, -1, 1, 2)
 ELECTRON_OF_SLOT = (0, 3, 1, 2)
 UNIT = 4
-TAIL = 2
-DIRECT = 1
 SHIFT = (5, 2)
 FIRST = {"wholes": (1, 3, 6, 9, 11), "parts": (4, 7, 9, 12, 14), "fourth": 6, "negate": (10, 14, 18)}
 PRODUCTS = {
@@ -24,7 +22,7 @@
     return (1 - place // 4) * (1 - place * (3 - place) // 2)
 
 
-def gather_kernel(f_ref, cols, rows, acc, neg, xy_send, xy_recv, d_send, d_recv, z_send, z_recv, z_tail, own_sem):
+def gather_kernel(f_ref, cols, rows, acc, neg, xy_send, xy_recv, d_send, d_recv, z_send, z_recv, own_sem):
     e, half, quarter = f_ref.shape[1], f_ref.shape[1] // 2, f_ref.shape[1] * 2 // UNIT
     r, z, s = lax.axis_index("row"), lax.axis_index("col"), lax.axis_index("slab")
     x, y_lo, core = r // 4, (r // 2) % 2, r % 2
@@ -39,12 +37,7 @@
         (1, 1): at(x, (y + 1) % 4, z, core),
         (1, -1): at(x, (y + 3) % 4, z, core),
         (2, 1): at(x, y, (z + 1) % 8, core),
-        (2, 2): at(x, y, (z + 2) % 8, core),
-        (2, 3): at(x, y, (z + 3) % 8, core),
-        (2, 4): at(x, y, (z + 4) % 8, core),
         (2, -1): at(x, y, (z + 7) % 8, core),
-        (2, -2): at(x, y, (z + 6) % 8, core),
-        (2, -3): at(x, y, (z + 5) % 8, core),
         "core": at(x, y, z, 1 - core),
     }
 
@@ -115,17 +108,17 @@
     def slot_of(c, place):
         return (c + (c + 2) // 3 - 3 * (c // 3) + 2 * is_end(place)) % 4
 
-    def z_copy(way, n, src, dst, sem, hops=1):
+    def z_copy(way, n, src, dst, sem):
         return pltpu.make_async_remote_copy(
             src_ref=src, dst_ref=dst, send_sem=sem, recv_sem=z_recv.at[way * 4 * UNIT + n],
-            device_id=to[(2, hops if way == 0 or hops == 4 else -hops)], device_id_type=MESH,
+            device_id=to[(2, 1 - 2 * way)], device_id_type=MESH,
         )
 
     def rows_part(plane, other, slot, q):
         return rows.at[plane, other * 4 + slot, pl.ds(pl.multiple_of(q * quarter, quarter), quarter)]
 
-    def there(way, hops):
-        return (j + (hops if way == 0 else 8 - hops)) % 8
+    def there(way):
+        return (j + (1 if way == 0 else 7)) % 8
 
     def z_own(other, planes):
         for way in (0, 1):
@@ -137,11 +130,10 @@
                         src = f_ref.at[plane] if other == 0 else whole(plane, (0, 2))
                         z_copy(
                             way, other * 2 * UNIT + i, src.at[pl.ds(q * quarter, quarter)],
-                            rows_part(plane, other, slot_of(j, there(way, 1)), q), z_send.at[way * 2],
+                            rows_part(plane, other, slot_of(j, there(way)), q), z_send.at[way * 2],
                         ).start()
 
     def z_step(slot):
-        last, direct = 4 * UNIT - TAIL, 4 * UNIT - DIRECT
         for way in (0, 1):
             place = places[way]
             back = (place + 7) % 8
@@ -157,37 +149,22 @@
                 block = rows_part(plane, other, slot_of(electron, j), q)
                 z_copy(way, n, block, block, z_send.at[0]).wait_recv()
 
-                def send(n, sem, hops=1):
-                    to_block = rows_part(plane, other, slot_of(electron, there(way, hops)), q)
-                    z_copy(way, n, block, to_block, sem, hops).start()
+                def send(n, sem):
+                    to_block = rows_part(plane, other, slot_of(electron, there(way)), q)
+                    z_copy(way, n, block, to_block, sem).start()
 
                 @pl.when((place >= 4) & (a == 0))
                 def _():
                     send(n, z_send.at[way * 2])
 
-                @pl.when((place >= 4) & (place <= 6) & (a == 1) & (n < last))
+                @pl.when((place >= 4) & (place <= 6) & (a == 1))
                 def _():
                     send(n, z_send.at[way * 2 + 1])
 
-                @pl.when((place >= 1) & (place <= 3) & (a == 0) & ((place < 3) | (n < last - UNIT)))
+                @pl.when((place >= 1) & (place <= 3) & (a == 0))
                 def _():
                     send(n + UNIT, z_send.at[way * 2 + 1])
 
-                if slot >= last - UNIT:
-
-                    @pl.when(((place == 4) | (place == 6)) & (n >= last) & (n < direct))
-                    def _():
-                        send(n, z_tail.at[way])
-
-                    @pl.when((place == 3) & (a == 0) & (n >= last - UNIT))
-                    def _():
-                        send(n + UNIT, z_tail.at[way])
-                        send(n + UNIT, z_tail.at[way], 3)
-
-                        @pl.when(n >= direct - UNIT)
-                        def _():
-                            send(n + UNIT, z_tail.at[way], 2)
-                            send(n + UNIT, z_tail.at[way], 4)
 
     def wait_columns(dx):
         pltpu.make_async_copy(cols.at[0, pl.ds(0, 8)], cols.at[0, pl.ds(0, 8)], d_recv.at[dx % 4]).wait()
@@ -290,21 +267,9 @@
     for way in (0, 1):
         drain(4, z_send.at[way * 2])
 
-        @pl.when((places[way] == 1) | (places[way] == 2))
+        @pl.when((places[way] >= 1) & (places[way] <= 6))
         def _():
             drain(4, z_send.at[way * 2 + 1])
-
-        @pl.when((places[way] >= 3) & (places[way] <= 6))
-        def _():
-            drain(3, z_send.at[way * 2 + 1])
-
-        @pl.when(places[way] == 3)
-        def _():
-            drain(3, z_tail.at[way])
-
-        @pl.when((places[way] == 4) | (places[way] == 6))
-        def _():
-            pltpu.make_async_copy(part(0, here, 0), part(0, here, 0), z_tail.at[way]).wait()
 
 
 def finish_kernel(cols, rows, acc, out, neg, last, acc_sem, last_sem):
@@ -369,7 +334,6 @@
             pltpu.SemaphoreType.DMA((4,)),
             pltpu.SemaphoreType.DMA((4,)),
             pltpu.SemaphoreType.DMA((8 * UNIT,)),
-            pltpu.SemaphoreType.DMA((2,)),
             pltpu.SemaphoreType.DMA((4,)),
         ],
         compiler_params=pltpu.CompilerParams(collective_id=0, has_side_effects=True, vmem_limit_bytes=20 * 2**20),

time: 52.8 us -> 50 us (0.947)
  Pallas kernels: 52.6 us -> 49.4 us
    pallas_call x1, Pallas kernels: 48.4 us -> 45.3 us  [body(): pl.pallas_call(gather_kernel, out_shape=(pltpu.VMEM((2, 32, e, pixels), j...]
where the time goes in v3:
time: 50 us; the launch traced here: 49.5 us
  Pallas kernels  49.4 us (99%)
    pallas_call x1, Pallas kernels, body(): pl.pallas_call(gather_kernel, out_shape=(pltpu.VMEM((2, 32, e, pixels), j...  45.3 us
    pallas_call x1, Pallas kernels, body(): pl.pallas_call(finish_kernel, out_shape=jax.ShapeDtypeStruct((2, 8 * e, 3...  4.11 us

profile of v3, /device:TPU:24, one launch (start us, length us, event | category | flops | bytes accessed | tf_op | source)
XLA Modules:
  0.0 49.5 jit_solution(6344162724374487359)
XLA Ops:
  0.0 45.3 %shard_map.17 = (bf16[2,32,64,1024]{3,2,1,0:T(8,128)(2,1)S(1)}, bf16[2,8,64,1024]{3,2,1,0:T(8,128)(2,1)S(1)}, f32[2,384,2048]{2,1,0:T(8,128)S(1)}) custom-call(bf16[2,64,1024]{2,1,0:T(8,128)(2,1)} %f_ref.1), custom_call_target="tpu_custom_call" | custom-call | flops 6442450944 | bytes 8388608 | tf_op jit(solution)/shard_map/pallas_call | solution.py:320
  45.3 4.1 %shard_map.18 = f32[2,512,2048]{2,1,0:T(8,128)} custom-call(bf16[2,32,64,1024]{3,2,1,0:T(8,128)(2,1)S(1)} %get-tuple-element.8.cols, bf16[2,8,64,1024]{3,2,1,0:T(8,128)(2,1)S(1)} %get-tuple-element.9.rows, f32[2,384,2048]{2,1,0:T(8,128)S(1)} %get-tuple-element.10.acc), custom_call_target="tpu_custom_call" | custom-call | flops 2147483648 | bytes 8388608 | tf_op jit(solution)/shard_map/pallas_call | solution.py:343

commit v4 on v3

--- a/solution.py
+++ b/solution.py
@@ -9,12 +9,12 @@
 NT = (((1,), (1,)), ((), ()))
 STEPS = (0, -1, 1, 2)
 ELECTRON_OF_SLOT = (0, 3, 1, 2)
-UNIT = 4
-SHIFT = (5, 2)
-FIRST = {"wholes": (1, 3, 6, 9, 11), "parts": (4, 7, 9, 12, 14), "fourth": 6, "negate": (10, 14, 18)}
+UNIT = 8
+SHIFT = (4, 1)
+FIRST = {"wholes": (3, 7, 13, 19, 23), "parts": (10, 15, 20, 25, 29), "fourth": 13, "negate": (20, 28, 36)}
 PRODUCTS = {
-    10: ((0, 2, 0),), 14: ((2, 2, 0),), 15: ((0, 4, -1),), 16: ((0, 4, 1),), 17: ((0, 4, 2),),
-    18: ((4, 2, 0),), 19: ((4, 2, -1),), 20: ((4, 2, 1),), 21: ((4, 2, 2),),
+    20: ((0, 2, 0),), 28: ((2, 2, 0),), 30: ((0, 4, -1),), 32: ((0, 4, 1),), 34: ((0, 4, 2),),
+    36: ((4, 2, 0),), 38: ((4, 2, -1),), 40: ((4, 2, 1),), 42: ((4, 2, 2),),
 }
 
 
@@ -295,16 +295,16 @@
     neg[...] = -rows[1, 6:8]
     left = jnp.concatenate([rows[0, 6:8].reshape(m, -1), neg[...].reshape(m, -1)])
     cross = jnp.concatenate([rows[1, 6:8].reshape(m, -1), rows[0, 6:8].reshape(m, -1)])
-    for block in range(4):
-        right_re = cols[0, block * 8 : block * 8 + 8].reshape(8 * e, -1)
-        right_im = cols[1, block * 8 : block * 8 + 8].reshape(8 * e, -1)
+    for block, (low, width) in enumerate(((0, 16), (16, 8), (24, 8))):
+        right_re = cols[0, low : low + width].reshape(width * e, -1)
+        right_im = cols[1, low : low + width].reshape(width * e, -1)
         sums = lax.dot_general(left, right_re, NT, preferred_element_type=jnp.float32) + lax.dot_general(
             cross, right_im, NT, preferred_element_type=jnp.float32
         )
         for plane in (0, 1):
-            last[plane, :, block * 8 * e : (block + 1) * 8 * e] = sums[plane * m : (plane + 1) * m]
+            last[plane, :, low * e : (low + width) * e] = sums[plane * m : (plane + 1) * m]
             for i in (0, 1):
-                lanes = pl.ds(block * 8 * e, 8 * e)
+                lanes = pl.ds(low * e, width * e)
                 copies.append(pltpu.make_async_copy(
                     last.at[plane, pl.ds(i * e, e), lanes], out.at[plane, place(6 + i), lanes],
                     last_sem.at[block * 4 + plane * 2 + i],
@@ -349,7 +349,7 @@
             pltpu.VMEM((2, e, pixels), jnp.bfloat16),
             pltpu.VMEM((2, 2 * e, 32 * e), jnp.float32),
             pltpu.SemaphoreType.DMA((12,)),
-            pltpu.SemaphoreType.DMA((16,)),
+            pltpu.SemaphoreType.DMA((12,)),
         ],
         compiler_params=pltpu.CompilerParams(vmem_limit_bytes=20 * 2**20),
         cost_estimate=pl.CostEstimate(flops=2 * 8 * e * 32 * e * pixels, bytes_accessed=2**23, transcendentals=0),

time: 50 us -> 50 us (level)
  no operation moved by 1% of the time
where the time goes in v4:
time: 50 us; the launch traced here: 49.8 us
  Pallas kernels  49.6 us (99%)
    pallas_call x1, Pallas kernels, body(): pl.pallas_call(gather_kernel, out_shape=(pltpu.VMEM((2, 32, e, pixels), j...  45.2 us
    pallas_call x1, Pallas kernels, body(): pl.pallas_call(finish_kernel, out_shape=jax.ShapeDtypeStruct((2, 8 * e, 3...  4.35 us

profile of v4, /device:TPU:24, one launch (start us, length us, event | category | flops | bytes accessed | tf_op | source)
XLA Modules:
  0.0 49.8 jit_solution(14934138633655733166)
XLA Ops:
  0.0 45.2 %shard_map.17 = (bf16[2,32,64,1024]{3,2,1,0:T(8,128)(2,1)S(1)}, bf16[2,8,64,1024]{3,2,1,0:T(8,128)(2,1)S(1)}, f32[2,384,2048]{2,1,0:T(8,128)S(1)}) custom-call(bf16[2,64,1024]{2,1,0:T(8,128)(2,1)} %f_ref.1), custom_call_target="tpu_custom_call" | custom-call | flops 6442450944 | bytes 8388608 | tf_op jit(solution)/shard_map/pallas_call | solution.py:320
  45.3 4.4 %shard_map.18 = f32[2,512,2048]{2,1,0:T(8,128)} custom-call(bf16[2,32,64,1024]{3,2,1,0:T(8,128)(2,1)S(1)} %get-tuple-element.8.cols, bf16[2,8,64,1024]{3,2,1,0:T(8,128)(2,1)S(1)} %get-tuple-element.9.rows, f32[2,384,2048]{2,1,0:T(8,128)S(1)} %get-tuple-element.10.acc), custom_call_target="tpu_custom_call" | custom-call | flops 2147483648 | bytes 8388608 | tf_op jit(solution)/shard_map/pallas_call | solution.py:343
